TPU v7x, 256 devices: a whole 4x4x8 slice. The times are simulated.
256 devices in a mesh: section: 16 (over x, y), tensor: 16 (over z, core).
Axes of the slice: x: 4, y: 4, z: 8, core: 2. Of those that a mesh axis runs over, the one named last changes fastest.
Arguments:
- queries: bfloat16 [16, 512, 8192], P('section', None, 'tensor'), may hold values from -20 to 20
- key_rows: bfloat16 [16, 512, 1024], P('section'), may hold values from -6 to 6
- value_rows: bfloat16 [16, 512, 1024], P('section'), may hold values from -6 to 6
- out_grad: bfloat16 [16, 512, 8192], P('section', None, 'tensor'), may hold values from -24 to 24
- layer_input: bfloat16 [16, 512, 8192], P('section', 'tensor'), may hold values from -64 to 64
- query_weight: bfloat16 [16, 8192, 8192], P('section', None, 'tensor'), may hold values from -0.0625 to 0.0625
- dion_basis: float32 [16, 8192, 256], P('section', 'tensor'), may hold values from -0.0625 to 0.0625
- lengths: int32 [16, 3], P('section'), may hold values from 1 to 256, 512 in all within a row
Outputs:
- upstream: bfloat16 [16, 512, 8192], P('section', 'tensor')
- left_factor: float32 [16, 8192, 256], P('section', 'tensor')
- right_factor: float32 [16, 8192, 256], P('section', 'tensor')
Inputs may be any that keep to these rules, and one draw needn't show every extreme that they name: For each section the lengths of the prompt, the chosen and the rejected response, in that order, summing to 512.
All inputs are finite; a program needn't handle non-finite values.
Results may differ from a plain program's by a relative error of at most 0.022.
Values may be sent and summed in bfloat16 or wider, within the bound.
No kernel may reach another device: no remote copies, remote signals or barrier semaphores. Data moves between devices by JAX's collectives and lax.ppermute only.
A program may use at most 64 MiB of HBM per device.

v0:
```python
import math
import jax
import jax.numpy as jnp
from jax import lax
from jax.sharding import PartitionSpec as P

D = 8192
HD = 128
GROUP = 8
rope_base = 500000.0
highest = lax.Precision.HIGHEST


def shifted(value, axis, steps):
    count = lax.axis_size(axis)
    first, last = (max(0, -steps), min(count, count - steps))
    return lax.ppermute(value, axis, [(source, source + steps) for source in range(first, last)])


def tree_layout(lengths_row, token_count):
    token_ids = jnp.arange(token_count, dtype=jnp.int32)
    bound_one = lengths_row[0]
    bound_two = lengths_row[0] + lengths_row[1]
    positions = jnp.where(token_ids < bound_two, token_ids, token_ids - lengths_row[1]).astype(
        jnp.float32
    )
    row_ids = token_ids[:, None]
    col_ids = token_ids[None, :]
    crossed = (row_ids >= bound_two) & (col_ids >= bound_one) & (col_ids < bound_two)
    visible = (col_ids <= row_ids) & jnp.logical_not(crossed)
    return (positions, visible)


def unrotate(rotated, positions):
    head_dim = rotated.shape[-1]
    half_dim = head_dim // 2
    freq_ids = jnp.arange(half_dim, dtype=jnp.float32)
    inverse = jnp.exp(-math.log(rope_base) * 2.0 * freq_ids / head_dim)
    angles = positions[:, None] * inverse[None, :]
    cosine = jnp.cos(angles)[:, None, :]
    sine_part = jnp.sin(angles)[:, None, :]
    first_half = rotated[..., :half_dim]
    second_half = rotated[..., half_dim:]
    return jnp.concatenate(
        [
            first_half * cosine + second_half * sine_part,
            second_half * cosine - first_half * sine_part,
        ],
        axis=-1,
    )


def local_backward(query_heads, grad_heads, key_block, value_block, visible):
    score_scale = 1.0 / math.sqrt(query_heads.shape[-1])
    scores = (
        jnp.einsum("qhd,kd->hqk", query_heads, key_block, preferred_element_type=jnp.float32)
        * score_scale
    )
    scores = jnp.where(visible[None], scores, -jnp.inf)
    row_max = jnp.max(scores, axis=-1, keepdims=True)
    exp_scores = jnp.exp(scores - row_max)
    weights = exp_scores / jnp.sum(exp_scores, axis=-1, keepdims=True)
    weights_low = weights.astype(jnp.bfloat16)
    outputs = jnp.einsum(
        "hqk,kd->qhd", weights_low, value_block, preferred_element_type=jnp.float32
    )
    out_dot = jnp.sum(grad_heads.astype(jnp.float32) * outputs, axis=-1)
    prob_grad = jnp.einsum(
        "qhd,kd->hqk", grad_heads, value_block, preferred_element_type=jnp.float32
    )
    score_grad = (weights * (prob_grad - out_dot.T[:, :, None])).astype(jnp.bfloat16)
    return (
        jnp.einsum("hqk,kd->qhd", score_grad, key_block, preferred_element_type=jnp.float32)
        * score_scale
    )


def local(queries, key_rows, value_rows, out_grad, layer_input, query_weight, dion_basis, lengths):
    token_count = queries.shape[1]
    local_width = queries.shape[2]
    local_heads = local_width // HD
    tensor_count = lax.axis_size("tensor")
    tensor_index = lax.axis_index("tensor")
    col_width = D // tensor_count
    gathered = lax.all_gather(layer_input[0], "tensor", axis=0, tiled=True)
    columns = lax.dynamic_slice_in_dim(gathered, tensor_index * col_width, col_width, 1)
    positions, visible = tree_layout(lengths[0], token_count)
    group_head = tensor_index * local_heads // GROUP
    key_block = lax.dynamic_slice_in_dim(key_rows[0], group_head * HD, HD, 1)
    value_block = lax.dynamic_slice_in_dim(value_rows[0], group_head * HD, HD, 1)
    rotated = local_backward(
        queries[0].reshape(token_count, local_heads, HD),
        out_grad[0].reshape(token_count, local_heads, HD),
        key_block,
        value_block,
        visible,
    )
    query_grad = unrotate(rotated, positions).reshape(token_count, local_width).astype(jnp.bfloat16)
    weight_local = query_weight[0]
    layer_grad = lax.psum_scatter(
        lax.dot_general(
            query_grad, weight_local, (((1,), (1,)), ((), ())), preferred_element_type=jnp.float32
        ).astype(jnp.bfloat16),
        "tensor",
        scatter_dimension=0,
        tiled=True,
    )
    upstream = shifted(layer_grad, "section", -1)
    grad_wide = query_grad.astype(jnp.float32)
    projected = lax.psum(jnp.dot(grad_wide, dion_basis[0], precision=highest), "tensor")
    column_wide = columns.astype(jnp.float32)
    left_raw = lax.dot_general(column_wide, projected, (((0,), (0,)), ((), ())), precision=highest)
    gram_part = lax.dot_general(left_raw, left_raw, (((0,), (0,)), ((), ())), precision=highest)
    mixed_part = jnp.dot(column_wide, left_raw, precision=highest)
    gram_total, mixed_total = lax.psum((gram_part, mixed_part), "tensor")
    lower_factor = jnp.linalg.cholesky(gram_total)
    left_orth = lax.linalg.triangular_solve(
        lower_factor, left_raw, left_side=False, lower=True, transpose_a=True
    )
    mixed_orth = lax.linalg.triangular_solve(
        lower_factor, mixed_total, left_side=False, lower=True, transpose_a=True
    )
    right_factor = lax.dot_general(
        grad_wide, mixed_orth, (((0,), (0,)), ((), ())), precision=highest
    )
    return (upstream[None], (left_orth * math.sqrt(D))[None], right_factor[None])


def solution(mesh):
    placed = (
        P("section", None, "tensor"),
        P("section", None, None),
        P("section", None, None),
        P("section", None, "tensor"),
        P("section", "tensor", None),
        P("section", None, "tensor"),
        P("section", "tensor", None),
        P("section", None),
    )
    return jax.shard_map(
        local,
        mesh=mesh,
        in_specs=placed,
        out_specs=(
            P("section", "tensor", None),
            P("section", "tensor", None),
            P("section", "tensor", None),
        ),
        check_vma=False,
    )
```

profile of v0, /device:TPU:26, one launch (start us, length us, event | category | flops | bytes accessed | tf_op | source)
XLA Modules:
  0.0 409.4 jit_solution(8106175779800506039)
XLA Ops:
  7.2 1.3 fusion.63
  11.2 1.2 reshape_squeeze.6
  12.4 0.7 fusion.27
  13.4 2.1 fusion.64
  15.5 1.9 copy-done.3
  17.4 1.4 fusion.5
  19.2 1.2 reshape_squeeze.7
  21.1 3.5 fusion.12
  25.4 1.5 fusion.19
  27.0 0.7 all-gather.3.cloned.1.call-update
  27.7 111.7 %all-reduce.5.cloned.1.call-done = f32[512,256]{1,0:T(8,128)} async-done(((f32[512,256]{1,0:T(8,128)}), f32[512,256]{1,0:T(8,128)}) %all-reduce.5.cloned.1.call-update) | async-done | bytes 524304 | tf_op jit(solution)/shard_map/psum | solution.py:110
  139.4 58.2 %all-gather.3.cloned.1.call-done = bf16[1,512,8192]{2,1,0:T(8,128)(2,1)} async-done(((bf16[1,32,8192]{2,1,0:T(8,128)(2,1)}), bf16[1,512,8192]{2,1,0:T(8,128)(2,1)}) %all-gather.3.cloned.1.call-update) | async-done | bytes 8388624 | tf_op jit(solution)/shard_map/all_gather | solution.py:85
  197.7 1.9 fusion.23
  199.6 1.7 fusion.65
  201.3 2.5 fusion.21
  203.9 10.2 %convolution_convert_fusion = bf16[512,8192]{1,0:T(8,128)(2,1)} fusion(bf16[512,512]{0,1:T(8,128)(2,1)S(1)} %bitcast.114, bf16[1,8192,512]{2,1,0:T(8,128)(2,1)} %param.15), kind=kOutput, calls=%fused_computation.3 | convolution fusion | flops 4299161600 | bytes 17301504 | tf_op jit(solution)/shard_map/dot_general | solution.py:101
  214.1 99.1 %all-reduce.7.cloned.1.call-done = (f32[256,256]{0,1:T(8,128)}, f32[512,256]{1,0:T(8,128)}) async-done(((f32[256,256]{0,1:T(8,128)}, f32[512,256]{1,0:T(8,128)}), (f32[256,256]{0,1:T(8,128)}, f32[512,256]{1,0:T(8,128)})) %all-reduce.7.cloned.1.call-update) | async-done | bytes 786448 | tf_op jit(solution)/shard_map/psum | solution.py:115
  313.3 1.1 copy.22
  314.4 1.0 fusion.35
  315.4 11.7 %cholesky.50 = f32[128,128]{1,0:T(8,128)S(1)} custom-call(f32[128,128]{1,0:T(8,128)S(1)} %cholesky.118), custom_call_target="Cholesky" | custom-call | tf_op jit(solution)/shard_map/jit(cholesky)/cholesky | solution.py:116
  327.2 9.8 %custom-call.14 = f32[1,128,128]{1,2,0:T(8,128)S(1)} custom-call(f32[1,128,128]{2,1,0:T(8,128)S(1)} %get-tuple-element.43), custom_call_target="InvertDiagBlocksLowerTriangular" | custom-call | tf_op jit(solution)/shard_map/jit(cholesky)/cholesky | solution.py:116
  337.5 11.7 %cholesky.105 = f32[128,128]{1,0:T(8,128)S(1)} custom-call(f32[128,128]{1,0:T(8,128)S(1)} %convolution_subtract_fusion.2), custom_call_target="Cholesky" | custom-call | tf_op jit(solution)/shard_map/jit(cholesky)/cholesky | solution.py:116
  351.9 4.0 while.4
  352.5 1.4 bitcast_dynamic-update-slice_fusion.2
  354.5 1.4 bitcast_dynamic-update-slice_fusion.2
  355.9 19.9 %custom-call.16 = f32[2,128,128]{1,2,0:T(8,128)S(1)} custom-call(f32[2,128,128]{2,1,0:T(8,128)S(1)} %get-tuple-element.18), custom_call_target="InvertDiagBlocksLowerTriangular" | custom-call | tf_op jit(solution)/shard_map/triangular_solve/custom-call.0 | solution.py:117
  377.3 1.0 copy.23
  378.8 8.2 %reduce-scatter.2.cloned.1.call-done = bf16[32,8192]{1,0:T(8,128)(2,1)} async-done(((bf16[512,8192]{1,0:T(8,128)(2,1)}), bf16[32,8192]{1,0:T(8,128)(2,1)}) %reduce-scatter.2.cloned.1.call-update) | async-done | bytes 524304 | tf_op jit(solution)/shard_map/reduce_scatter | solution.py:100
  387.0 2.8 collective-permute-start
  390.8 1.4 convolution_bitcast_fusion
  392.2 9.8 %collective-permute-done = bf16[32,8192]{1,0:T(8,128)(2,1)S(1)} collective-permute-done((bf16[32,8192]{1,0:T(8,128)(2,1)}, bf16[32,8192]{1,0:T(8,128)(2,1)S(1)}, u32[]{:S(2)}, u32[]{:S(2)}) %collective-permute-start) | collective-permute-done | bytes 524320 | tf_op jit(solution)/shard_map/ppermute | solution.py:17
  402.1 0.8 copy.50
  (48 shorter events, 9.6 us)
Async XLA Ops:
  7.2 5.2 %copy-start = (bf16[1,512,1024]{2,1,0:T(8,128)(2,1)S(1)}, bf16[1,512,1024]{2,1,0:T(8,128)(2,1)}, u32[]{:S(2)}) copy-start(bf16[1,512,1024]{2,1,0:T(8,128)(2,1)} %param.11) | copy-start | bytes 3145732
  7.2 132.2 %all-reduce.5.cloned.1.call-start = ((), (), s32[]{:S(2)}) async-start(), calls=%async_computation.2 | async-start | bytes 1048576 | tf_op jit(solution)/shard_map/psum | solution.py:110
  15.5 1.9 copy-start.3
  21.1 4.2 %copy-start.1 = (f32[1,512,256]{2,1,0:T(8,128)S(1)}, f32[1,512,256]{2,1,0:T(8,128)}, u32[]{:S(2)}) copy-start(f32[1,512,256]{2,1,0:T(8,128)} %param.16) | copy-start | bytes 1572868
  26.9 170.7 %all-gather.3.cloned.1.call-start = ((), (), s32[]{:S(2)}) async-start(), calls=%async_computation.3 | async-start | bytes 8912896 | tf_op jit(solution)/shard_map/all_gather | solution.py:85
  27.7 285.6 %all-reduce.7.cloned.1.call-start = ((), (), s32[]{:S(2)}) async-start(), calls=%async_computation.4 | async-start | bytes 1572864 | tf_op jit(solution)/shard_map/psum | solution.py:115
  203.8 183.2 %reduce-scatter.2.cloned.1.call-start = ((), (), s32[]{:S(2)}) async-start(), calls=%async_computation.1 | async-start | bytes 8912896 | tf_op jit(solution)/shard_map/reduce_scatter | solution.py:100
  313.3 65.1 %copy-start.2 = (f32[512,256]{1,0:T(8,128)S(1)}, f32[512,256]{1,0:T(8,128)}, u32[]{:S(2)}) copy-start(f32[512,256]{1,0:T(8,128)} %get-tuple-element.35) | copy-start | bytes 1572868
  387.0 15.1 %collective-permute-start = (bf16[32,8192]{1,0:T(8,128)(2,1)}, bf16[32,8192]{1,0:T(8,128)(2,1)S(1)}, u32[]{:S(2)}, u32[]{:S(2)}) collective-permute-start(bf16[32,8192]{1,0:T(8,128)(2,1)} %reduce-scatter.2.cloned.1.call-done), channel_id=1, source_target_pairs={{16,0},{32,16},{48,32},{64,48},{80,64},{96,80},{112,96},{128,112},... | collective-permute-start | bytes 1572872 | tf_op jit(solution)/shard_map/ppermute | solution.py:17
Sparse Core Ops, SparseCore 0:
  27.1 112.3 all-reduce.4
  141.4 56.2 all-gather.2
  203.9 109.2 all-reduce.6
  315.7 71.2 reduce-scatter.1
where the time goes:
time: 410 us; the launch traced here: 409 us
  waiting for transfers between devices  288 us (70%)
  other arithmetic  60.6 us (15%)
  matrix products  28.2 us (7%)
  between operations  16.7 us (4%)
  local copies, waits for them, and re-layouts  13.1 us (3%)
    psum x1, waiting for transfers between devices, local(): lax.psum(jnp.dot(grad_wide, dion_basis[0], precision=highest), 'tensor')  112 us
    psum x1, waiting for transfers between devices, local(): gram_total, mixed_total = lax.psum((gram_part, mixed_part), 'tensor')  99.1 us
    all_gather x1, waiting for transfers between devices, local(): gathered = lax.all_gather(layer_input[0], 'tensor', axis=0, tiled=True)  58.2 us
    another operation x7, other arithmetic, local(): lower_factor = jnp.linalg.cholesky(gram_total)  34.6 us
    another operation x4, other arithmetic, local(): lax.linalg.triangular_solve(lower_factor, left_raw, left_side=False, lowe...  19.9 us
    dot_general x1, matrix products, local(): lax.dot_general(query_grad, weight_local, (((1,), (1,)), ((), ())), prefe...  10.2 us
    ppermute x1, waiting for transfers between devices, shifted(): lax.ppermute(value, axis, [(source, source + steps) for source in range(f...  9.81 us
    reduce_scatter x1, waiting for transfers between devices, local(): lax.psum_scatter(lax.dot_general(query_grad, weight_local, (((1,), (1,)),...  8.25 us
  transfers between devices with their start and end apart: 5, of which 5 were waited for; matrix products, arithmetic and copies ran while one was open for 19% of the time, Pallas kernels for 0%

commit v1 on v0

--- a/solution.py
+++ b/solution.py
@@ -107,7 +107,9 @@
     )
     upstream = shifted(layer_grad, "section", -1)
     grad_wide = query_grad.astype(jnp.float32)
-    projected = lax.psum(jnp.dot(grad_wide, dion_basis[0], precision=highest), "tensor")
+    projected = jnp.sum(
+        lax.all_gather(jnp.dot(grad_wide, dion_basis[0], precision=highest), "tensor"), axis=0
+    )
     column_wide = columns.astype(jnp.float32)
     left_raw = lax.dot_general(column_wide, projected, (((0,), (0,)), ((), ())), precision=highest)
     gram_part = lax.dot_general(left_raw, left_raw, (((0,), (0,)), ((), ())), precision=highest)

time: 410 us -> 355 us (0.87)
  waiting for transfers between devices: 288 us -> 229 us
    psum x1 -> x0, waiting for transfers between devices: 112 us -> none  [local(): lax.psum(jnp.dot(grad_wide, dion_basis[0], precision=highest), 'tensor')]
    all_gather x0 -> x1, waiting for transfers between devices: none -> 58 us  [local(): lax.all_gather(jnp.dot(grad_wide, dion_basis[0], precision=highest), 'ten...]
    all_gather x1, waiting for transfers between devices: 58.2 us -> 52.3 us  [local(): gathered = lax.all_gather(layer_input[0], 'tensor', axis=0, tiled=True)]
  transfers between devices with their start and end apart: 5 -> 5, of which waited for: 5 -> 5; matrix products, arithmetic and copies ran while one was open for 19% -> 23% of each run, Pallas kernels for 0% -> 0%
where the time goes in v1:
time: 355 us; the launch traced here: 354 us
  waiting for transfers between devices  229 us (65%)
  other arithmetic  64.6 us (18%)
  matrix products  28 us (8%)
  between operations  16.7 us (5%)
  local copies, waits for them, and re-layouts  13.1 us (4%)
    psum x1, waiting for transfers between devices, local(): gram_total, mixed_total = lax.psum((gram_part, mixed_part), 'tensor')  99.3 us
    all_gather x1, waiting for transfers between devices, local(): lax.all_gather(jnp.dot(grad_wide, dion_basis[0], precision=highest), 'ten...  58 us
    all_gather x1, waiting for transfers between devices, local(): gathered = lax.all_gather(layer_input[0], 'tensor', axis=0, tiled=True)  52.3 us
    another operation x7, other arithmetic, local(): lower_factor = jnp.linalg.cholesky(gram_total)  34.6 us
    another operation x4, other arithmetic, local(): lax.linalg.triangular_solve(lower_factor, left_raw, left_side=False, lowe...  19.9 us
    dot_general x1, matrix products, local(): lax.dot_general(query_grad, weight_local, (((1,), (1,)), ((), ())), prefe...  10.2 us
    ppermute x1, waiting for transfers between devices, shifted(): lax.ppermute(value, axis, [(source, source + steps) for source in range(f...  9.75 us
    reduce_scatter x1, waiting for transfers between devices, local(): lax.psum_scatter(lax.dot_general(query_grad, weight_local, (((1,), (1,)),...  8.64 us
  transfers between devices with their start and end apart: 5, of which 5 were waited for; matrix products, arithmetic and copies ran while one was open for 23% of the time, Pallas kernels for 0%

profile of v1, /device:TPU:26, one launch (start us, length us, event | category | flops | bytes accessed | tf_op | source)
XLA Modules:
  0.0 354.1 jit_solution(5321891218017696644)
XLA Ops:
  7.2 1.3 fusion.63
  11.2 1.2 reshape_squeeze.6
  12.4 0.7 fusion.27
  13.4 2.1 fusion.64
  15.5 1.9 copy-done.3
  17.4 1.4 fusion.5
  19.2 1.2 reshape_squeeze.7
  21.1 3.5 fusion.12
  25.4 1.5 fusion.19
  27.7 58.0 %all-gather.7.cloned.1.call-done = f32[8192,256]{1,0:T(8,128)} async-done(((f32[512,256]{1,0:T(8,128)}), f32[8192,256]{1,0:T(8,128)}) %all-gather.7.cloned.1.call-update) | async-done | bytes 8388624 | tf_op jit(solution)/shard_map/all_gather | solution.py:111
  85.7 4.0 %reduce_sum.29 = f32[512,256]{1,0:T(8,128)S(1)} reduce(f32[16,512,256]{2,1,0:T(8,128)} %bitcast.114, f32[]{:T(128)} %constant.112.clone.1), dimensions={0}, to_apply=%region_4.5 | reduce | flops 1966080 | bytes 8912900 | tf_op jit(solution)/shard_map/reduce_sum | solution.py:110
  89.7 52.3 %all-gather.5.cloned.1.call-done = bf16[1,512,8192]{2,1,0:T(8,128)(2,1)} async-done(((bf16[1,32,8192]{2,1,0:T(8,128)(2,1)}), bf16[1,512,8192]{2,1,0:T(8,128)(2,1)}) %all-gather.5.cloned.1.call-update) | async-done | bytes 8388624 | tf_op jit(solution)/shard_map/all_gather | solution.py:85
  142.0 1.8 fusion.23
  143.8 1.7 fusion.65
  145.5 2.5 fusion.21
  148.1 10.2 %convolution_convert_fusion = bf16[512,8192]{1,0:T(8,128)(2,1)} fusion(bf16[512,512]{0,1:T(8,128)(2,1)S(1)} %bitcast.116, bf16[1,8192,512]{2,1,0:T(8,128)(2,1)} %param.15), kind=kOutput, calls=%fused_computation.3 | convolution fusion | flops 4299161600 | bytes 17301504 | tf_op jit(solution)/shard_map/dot_general | solution.py:101
  158.4 99.3 %all-reduce.4.cloned.1.call-done = (f32[256,256]{0,1:T(8,128)}, f32[512,256]{1,0:T(8,128)}) async-done(((f32[256,256]{0,1:T(8,128)}, f32[512,256]{1,0:T(8,128)}), (f32[256,256]{0,1:T(8,128)}, f32[512,256]{1,0:T(8,128)})) %all-reduce.4.cloned.1.call-update) | async-done | bytes 786448 | tf_op jit(solution)/shard_map/psum | solution.py:117
  257.7 1.1 copy.22
  258.9 1.0 fusion.35
  259.9 11.7 %cholesky.50 = f32[128,128]{1,0:T(8,128)S(1)} custom-call(f32[128,128]{1,0:T(8,128)S(1)} %cholesky.118), custom_call_target="Cholesky" | custom-call | tf_op jit(solution)/shard_map/jit(cholesky)/cholesky | solution.py:118
  271.6 9.8 %custom-call.14 = f32[1,128,128]{1,2,0:T(8,128)S(1)} custom-call(f32[1,128,128]{2,1,0:T(8,128)S(1)} %get-tuple-element.43), custom_call_target="InvertDiagBlocksLowerTriangular" | custom-call | tf_op jit(solution)/shard_map/jit(cholesky)/cholesky | solution.py:118
  281.9 11.7 %cholesky.105 = f32[128,128]{1,0:T(8,128)S(1)} custom-call(f32[128,128]{1,0:T(8,128)S(1)} %convolution_subtract_fusion.2), custom_call_target="Cholesky" | custom-call | tf_op jit(solution)/shard_map/jit(cholesky)/cholesky | solution.py:118
  296.4 4.0 %while.4 = (s32[]{:T(128)}, f32[256,256]{1,0:T(8,128)S(1)}, s32[2,2]{1,0:T(2,128)S(1)}, f32[2,128,128]{2,1,0:T(8,128)S(1)}, s32[]{:T(128)}) while((s32[]{:T(128)}, f32[256,256]{1,0:T(8,128)S(1)}, s32[2,2]{1,0:T(2,128)S(1)}, f32[2,128,128]{2,1,0:T(8,128)S(1)}, s32[]{:T(128)}) %tuple.38), condition=%wide.while_cond, body=%wide.while_body.sunk | while | flops 2 | bytes 131181 | solution.py:119
  297.0 1.4 bitcast_dynamic-update-slice_fusion.2
  299.0 1.4 bitcast_dynamic-update-slice_fusion.2
  300.4 19.9 %custom-call.16 = f32[2,128,128]{1,2,0:T(8,128)S(1)} custom-call(f32[2,128,128]{2,1,0:T(8,128)S(1)} %get-tuple-element.18), custom_call_target="InvertDiagBlocksLowerTriangular" | custom-call | tf_op jit(solution)/shard_map/triangular_solve/custom-call.0 | solution.py:119
  321.8 1.0 copy.23
  323.2 8.6 %reduce-scatter.2.cloned.1.call-done = bf16[32,8192]{1,0:T(8,128)(2,1)} async-done(((bf16[512,8192]{1,0:T(8,128)(2,1)}), bf16[32,8192]{1,0:T(8,128)(2,1)}) %reduce-scatter.2.cloned.1.call-update) | async-done | bytes 524304 | tf_op jit(solution)/shard_map/reduce_scatter | solution.py:100
  331.8 2.7 collective-permute-start
  335.6 1.4 convolution_bitcast_fusion
  337.0 9.7 %collective-permute-done = bf16[32,8192]{1,0:T(8,128)(2,1)S(1)} collective-permute-done((bf16[32,8192]{1,0:T(8,128)(2,1)}, bf16[32,8192]{1,0:T(8,128)(2,1)S(1)}, u32[]{:S(2)}, u32[]{:S(2)}) %collective-permute-start) | collective-permute-done | bytes 524320 | tf_op jit(solution)/shard_map/ppermute | solution.py:17
  346.8 0.8 copy.49
  (49 shorter events, 10.3 us)
Async XLA Ops:
  7.2 5.2 %copy-start = (bf16[1,512,1024]{2,1,0:T(8,128)(2,1)S(1)}, bf16[1,512,1024]{2,1,0:T(8,128)(2,1)}, u32[]{:S(2)}) copy-start(bf16[1,512,1024]{2,1,0:T(8,128)(2,1)} %param.11) | copy-start | bytes 3145732
  7.2 78.5 %all-gather.7.cloned.1.call-start = ((), (), s32[]{:S(2)}) async-start(), calls=%async_computation.3 | async-start | bytes 8912896 | tf_op jit(solution)/shard_map/all_gather | solution.py:111
  15.5 1.9 copy-start.3
  21.1 4.2 %copy-start.1 = (f32[1,512,256]{2,1,0:T(8,128)S(1)}, f32[1,512,256]{2,1,0:T(8,128)}, u32[]{:S(2)}) copy-start(f32[1,512,256]{2,1,0:T(8,128)} %param.16) | copy-start | bytes 1572868
  26.9 115.1 %all-gather.5.cloned.1.call-start = ((), (), s32[]{:S(2)}) async-start(), calls=%async_computation.2 | async-start | bytes 8912896 | tf_op jit(solution)/shard_map/all_gather | solution.py:85
  27.7 230.0 %all-reduce.4.cloned.1.call-start = ((), (), s32[]{:S(2)}) async-start(), calls=%async_computation.4 | async-start | bytes 1572864 | tf_op jit(solution)/shard_map/psum | solution.py:117
  148.0 183.8 %reduce-scatter.2.cloned.1.call-start = ((), (), s32[]{:S(2)}) async-start(), calls=%async_computation.1 | async-start | bytes 8912896 | tf_op jit(solution)/shard_map/reduce_scatter | solution.py:100
  257.7 65.1 %copy-start.2 = (f32[512,256]{1,0:T(8,128)S(1)}, f32[512,256]{1,0:T(8,128)}, u32[]{:S(2)}) copy-start(f32[512,256]{1,0:T(8,128)} %get-tuple-element.35) | copy-start | bytes 1572868
  331.8 14.9 %collective-permute-start = (bf16[32,8192]{1,0:T(8,128)(2,1)}, bf16[32,8192]{1,0:T(8,128)(2,1)S(1)}, u32[]{:S(2)}, u32[]{:S(2)}) collective-permute-start(bf16[32,8192]{1,0:T(8,128)(2,1)} %reduce-scatter.2.cloned.1.call-done), channel_id=1, source_target_pairs={{16,0},{32,16},{48,32},{64,48},{80,64},{96,80},{112,96},{128,112},... | collective-permute-start | bytes 1572872 | tf_op jit(solution)/shard_map/ppermute | solution.py:17
Sparse Core Ops, SparseCore 0:
  27.1 58.6 all-gather.6
  87.5 54.4 all-gather.4
  148.2 109.5 all-reduce.3
  260.3 71.4 reduce-scatter.1
